TPU v7x, 32 devices: a whole 2x2x4 slice. The times are simulated.
32 devices in a mesh: sub: 1, pts: 32 (over z, y, x, core).
Axes of the slice: x: 2, y: 2, z: 4, core: 2. Of those that a mesh axis runs over, the one named last changes fastest.
Arguments:
- cam_jac: float32 [2, 9, 4, 32768], P(None, None, None, ('sub', 'pts')), may hold values from -3 to 3
- point_jac: float32 [2, 3, 4, 32768], P(None, None, None, ('sub', 'pts')), may hold values from -3 to 3
- residuals: float32 [2, 4, 32768], P(None, None, ('sub', 'pts')), may hold values from -6 to 6
- obs_camera: int32 [4, 32768], P(None, ('sub', 'pts')), may hold values from 0 to 4095
- damping: float32 [1], P('sub'), may hold values from 0.01 to 0.1
Outputs:
- camera_step: float32 [9, 4096], P(None, ('sub', 'pts'))
- point_step: float32 [3, 32768], P(None, ('sub', 'pts'))
All inputs are finite; a program needn't handle non-finite values.
Results may differ from a plain program's by a relative error of at most 0.00022.
Values sent between devices are 32-bit elements; how exact they have to be, the bound alone decides.
A program may use at most 64 MiB of HBM per device.

v0:
```python
import jax
import jax.numpy as jnp
from jax import lax
from jax.sharding import PartitionSpec as P

NCAM = 4096
ITERS = 3


low_width = 16


def cofactor(matrix, row, col):
    kept_rows = [other for other in range(3) if other != row]
    kept_cols = [other for other in range(3) if other != col]
    sign = 1.0 if (row + col) % 2 == 0 else -1.0
    first = matrix[kept_rows[0], kept_cols[0]] * matrix[kept_rows[1], kept_cols[1]]
    second = matrix[kept_rows[0], kept_cols[1]] * matrix[kept_rows[1], kept_cols[0]]
    return sign * (first - second)


def point_inverse(point_jac, damp_value):
    gram = jnp.sum(point_jac[:, :, None] * point_jac[:, None, :], axis=(0, 3))
    gram = gram + damp_value * jnp.eye(3, dtype=jnp.float32)[:, :, None]
    determinant = (
        gram[0, 0] * cofactor(gram, 0, 0)
        + gram[0, 1] * cofactor(gram, 0, 1)
        + gram[0, 2] * cofactor(gram, 0, 2)
    )
    adjugate = jnp.stack(
        [jnp.stack([cofactor(gram, col, row) for col in range(3)]) for row in range(3)]
    )
    return adjugate / determinant[None, None]


def block_length():
    return 512


def hot_tables(camera_ids, high_width):
    upper_ids = camera_ids // low_width
    lower_ids = camera_ids % low_width
    length = camera_ids.shape[0]
    hot_high = (lax.broadcasted_iota(jnp.int32, (high_width, length), 0) == upper_ids[None]).astype(
        jnp.float32
    )
    hot_low = (lax.broadcasted_iota(jnp.int32, (low_width, length), 0) == lower_ids[None]).astype(
        jnp.float32
    )
    return (hot_high, hot_low)


def gather_cameras(camera_field, obs_camera):
    fields, cameras = camera_field.shape
    high_width = cameras // low_width
    lookup = (
        camera_field.reshape(fields, high_width, low_width)
        .transpose(0, 2, 1)
        .reshape(fields * low_width, high_width)
    )
    flat_ids = obs_camera.reshape(-1)
    count = flat_ids.shape[0]
    length = block_length()

    def one_block(camera_ids):
        hot_high, hot_low = hot_tables(camera_ids, high_width)
        picked = jnp.dot(lookup, hot_high, precision=lax.Precision.HIGHEST).reshape(
            fields, low_width, length
        )
        return jnp.sum(picked * hot_low[None], axis=1)

    pieces = lax.map(one_block, flat_ids.reshape(count // length, length))
    return pieces.transpose(1, 0, 2).reshape((fields,) + obs_camera.shape)


def scatter_cameras(values, obs_camera, cameras):
    fields = values.shape[0]
    high_width = cameras // low_width
    flat_ids = obs_camera.reshape(-1)
    count = flat_ids.shape[0]
    length = block_length()
    blocks = count // length
    value_blocks = values.reshape(fields, blocks, length).transpose(1, 0, 2)

    def add_block(running, item):
        camera_ids, block_values = item
        hot_high, hot_low = hot_tables(camera_ids, high_width)
        weighted = (block_values[:, None, :] * hot_low[None]).reshape(fields * low_width, length)
        summed = lax.dot_general(
            weighted, hot_high, (((1,), (1,)), ((), ())), precision=lax.Precision.HIGHEST
        )
        return (running + summed, None)

    start = jnp.zeros((fields * low_width, high_width), jnp.float32)
    running, unused = lax.scan(add_block, start, (flat_ids.reshape(blocks, length), value_blocks))
    return (
        running.reshape(fields, low_width, high_width).transpose(0, 2, 1).reshape(fields, cameras)
    )


def predict(camera_field, cam_jac, obs_camera):
    at_obs = gather_cameras(camera_field, obs_camera)
    return jnp.sum(cam_jac * at_obs[None], axis=1)


def schur_terms(camera_field, cam_jac, point_jac, obs_camera, inverse, cameras):
    predicted = predict(camera_field, cam_jac, obs_camera)
    pulled = jnp.sum(point_jac * predicted[:, None], axis=(0, 2))
    solved = jnp.sum(inverse * pulled[None], axis=1)
    remain = predicted - jnp.sum(point_jac * solved[None, :, None], axis=1)
    return scatter_cameras(jnp.sum(cam_jac * remain[:, None], axis=0), obs_camera, cameras)


def body(cam_jac, point_jac, residuals, obs_camera, damping):
    damp_value = damping[0]
    cameras = NCAM
    params = cam_jac.shape[1]
    inverse = point_inverse(point_jac, damp_value)
    grad_point = jnp.sum(point_jac * residuals[:, None], axis=(0, 2))
    lifted = jnp.sum(inverse * grad_point[None], axis=1)
    remain = residuals - jnp.sum(point_jac * lifted[None, :, None], axis=1)
    stacked = jnp.concatenate(
        [jnp.sum(cam_jac * remain[:, None], axis=0), jnp.sum(cam_jac * cam_jac, axis=0)], axis=0
    )
    both_terms = scatter_cameras(stacked, obs_camera, cameras)
    right_terms = -both_terms[:params]
    diagonal_terms = both_terms[params:]
    right_side, diagonal = lax.psum((right_terms, diagonal_terms), "pts")
    precond = damp_value + diagonal
    solution = jnp.zeros_like(right_side)
    residual_vec = right_side
    scaled = residual_vec / precond
    direction = scaled
    norm_now = jnp.sum(residual_vec * scaled)
    for iteration in range(ITERS):
        summed = lax.psum(
            schur_terms(direction, cam_jac, point_jac, obs_camera, inverse, cameras), "pts"
        )
        image = damp_value * direction + summed
        step_size = norm_now / jnp.sum(direction * image)
        solution = solution + step_size * direction
        residual_vec = residual_vec - step_size * image
        if iteration + 1 < ITERS:
            scaled = residual_vec / precond
            norm_next = jnp.sum(residual_vec * scaled)
            direction = scaled + norm_next / norm_now * direction
            norm_now = norm_next
    per_device = cameras // lax.axis_size("pts")
    offset = lax.axis_index("pts") * per_device
    camera_step = lax.dynamic_slice_in_dim(solution, offset, per_device, 1)
    predicted = predict(solution, cam_jac, obs_camera)
    pulled = grad_point + jnp.sum(point_jac * predicted[:, None], axis=(0, 2))
    point_step = -jnp.sum(inverse * pulled[None], axis=1)
    return (camera_step, point_step)


def solution(mesh):
    in_specs = (
        P(None, None, None, ("sub", "pts")),
        P(None, None, None, ("sub", "pts")),
        P(None, None, ("sub", "pts")),
        P(None, ("sub", "pts")),
        P("sub"),
    )
    out_specs = (P(None, ("sub", "pts")), P(None, ("sub", "pts")))
    return jax.shard_map(body, mesh=mesh, in_specs=in_specs, out_specs=out_specs, check_vma=False)
```

profile of v0, /device:TPU:0, one launch (start us, length us, event | category | flops | bytes accessed | tf_op | source)
XLA Modules:
  0.0 602.2 jit_solution(17663560836401889620)
XLA Ops:
  7.9 1.1 multiply_reduce_fusion.13
  13.0 6.3 %while.104 = (s32[]{:T(128)}, f32[288,256]{1,0:T(8,128)S(1)}, f32[8,18,512]{2,0,1:T(8,128)S(1)}, s32[8,512]{1,0:T(8,128)S(1)}, s32[]{:T(128)}, /*index=5*/s32[]{:T(128)}) while((s32[]{:T(128)}, f32[288,256]{1,0:T(8,128)S(1)}, f32[8,18,512]{2,0,1:T(8,128)S(1)}, s32[8,512]{1,0:T(8,128)S(1)}, s32[]{:T(128)}, ...), condition=%wide.region_7.8_spmd.clone, body=%wide.region_6.7_spmd.clone.sunk | while | flops 453437440 | bytes 2033751 | solution.py:95
  20.0 1.6 fusion.21
  21.6 2.8 neg.10
  24.4 1.4 slice.37
  25.9 132.2 %all-reduce.12.cloned.1.call-done = (f32[9,4096]{1,0:T(8,128)}, f32[9,4096]{1,0:T(8,128)}) async-done(((f32[9,4096]{1,0:T(8,128)}, f32[9,4096]{1,0:T(8,128)}), (f32[9,4096]{1,0:T(8,128)}, f32[9,4096]{1,0:T(8,128)})) %all-reduce.12.cloned.1.call-update) | async-done | bytes 294928 | tf_op jit(solution)/shard_map/psum | solution.py:128
  159.9 4.0 while.100
  165.1 5.0 while.105
  170.5 1.4 reshape.764
  172.0 125.7 %all-reduce.6.cloned.1.call-done = f32[9,4096]{1,0:T(8,128)} async-done(((f32[9,4096]{1,0:T(8,128)}), f32[9,4096]{1,0:T(8,128)}) %all-reduce.6.cloned.1.call-update) | async-done | bytes 147472 | tf_op jit(solution)/shard_map/psum | solution.py:136
  297.7 1.7 multiply_reduce_fusion.18
  300.6 1.7 multiply_reduce_fusion.17
  304.4 4.0 while.101
  309.0 5.0 while.106
  314.4 1.4 reshape.769
  316.0 125.6 %all-reduce.8.cloned.1.call-done = f32[9,4096]{1,0:T(8,128)} async-done(((f32[9,4096]{1,0:T(8,128)}), f32[9,4096]{1,0:T(8,128)}) %all-reduce.8.cloned.1.call-update) | async-done | bytes 147472 | tf_op jit(solution)/shard_map/psum | solution.py:136
  441.6 1.7 multiply_reduce_fusion.16
  444.6 1.7 multiply_reduce_fusion.15
  448.6 4.0 while.102
  453.2 5.0 while.107
  458.6 1.4 reshape.774
  460.0 125.8 %all-reduce.10.cloned.1.call-done = f32[9,4096]{1,0:T(8,128)} async-done(((f32[9,4096]{1,0:T(8,128)}), f32[9,4096]{1,0:T(8,128)}) %all-reduce.10.cloned.1.call-update) | async-done | bytes 147472 | tf_op jit(solution)/shard_map/psum | solution.py:136
  585.8 1.7 multiply_reduce_fusion.14
  589.7 4.0 while.103
  (517 shorter events, 47.7 us)
Async XLA Ops:
  7.2 5.4 copy-start
  7.2 150.9 %all-reduce.12.cloned.1.call-start = ((), (), s32[]{:S(2)}) async-start(), calls=%async_computation.3 | async-start | bytes 1048576 | tf_op jit(solution)/shard_map/psum | solution.py:128
  10.1 2.6 copy-start.7
  10.2 2.8 copy-start.9
  21.6 2.8 copy-start.3
  25.8 271.9 %all-reduce.6.cloned.1.call-start = ((), (), s32[]{:S(2)}) async-start(), calls=%async_computation | async-start | bytes 524288 | tf_op jit(solution)/shard_map/psum | solution.py:136
  163.9 0.9 copy-start.1
  163.9 0.9 copy-start.6
  170.5 127.2 %copy-start.5 = (f32[9,4096]{1,0:T(8,128)S(1)}, f32[9,4096]{1,0:T(8,128)}, u32[]{:S(2)}) copy-start(f32[9,4096]{1,0:T(8,128)} %get-tuple-element.634) | copy-start | bytes 442372
  170.5 130.1 %copy-start.2 = (f32[9,4096]{1,0:T(8,128)S(1)}, f32[9,4096]{1,0:T(8,128)}, u32[]{:S(2)}) copy-start(f32[9,4096]{1,0:T(8,128)} %get-tuple-element.635) | copy-start | bytes 442372
  172.0 269.6 %all-reduce.8.cloned.1.call-start = ((), (), s32[]{:S(2)}) async-start(), calls=%async_computation.1 | async-start | bytes 524288 | tf_op jit(solution)/shard_map/psum | solution.py:136
  315.8 270.0 %all-reduce.10.cloned.1.call-start = ((), (), s32[]{:S(2)}) async-start(), calls=%async_computation.2 | async-start | bytes 524288 | tf_op jit(solution)/shard_map/psum | solution.py:136
  441.6 6.1 %copy-start.4 = (f32[9,4096]{1,0:T(8,128)S(1)}, f32[9,4096]{1,0:T(8,128)}, u32[]{:S(2)}) copy-start(f32[9,4096]{1,0:T(8,128)} %all-reduce.8.cloned.1.call-done) | copy-start | bytes 442372
  593.7 0.7 copy-start.8
Sparse Core Ops, SparseCore 0:
  25.9 132.0 all-reduce.11
  172.1 125.5 all-reduce.5
  315.9 125.6 all-reduce.7
  460.1 125.6 all-reduce.9
where the time goes:
time: 603 us; the launch traced here: 602 us
  waiting for transfers between devices  509 us (84%)
  matrix products  26.7 us (4%)
  other arithmetic  23.2 us (4%)
  between operations  21.5 us (4%)
  local copies, waits for them, and re-layouts  17.1 us (3%)
    psum x3, waiting for transfers between devices, body(): lax.psum(schur_terms(direction, cam_jac, point_jac, obs_camera, inverse,...  377 us
    psum x1, waiting for transfers between devices, body(): right_side, diagonal = lax.psum((right_terms, diagonal_terms), 'pts')  132 us
    dot_general x32, matrix products, add_block(): lax.dot_general(weighted, hot_high, (((1,), (1,)), ((), ())), precision=l...  16 us
  transfers between devices with their start and end apart: 4, of which 4 were waited for; matrix products, arithmetic and copies ran while one was open for 0% of the time, Pallas kernels for 0%

commit v1 on v0

v1 whole, which is shorter than its diff:
```python
import functools

import jax
import jax.numpy as jnp
from jax import lax
from jax.experimental import pallas as pl
from jax.experimental.pallas import tpu as pltpu
from jax.sharding import PartitionSpec as P

NCAM = 4096
ITERS = 3
NT = (((1,), (1,)), ((), ()))


def cofactor(matrix, row, col):
    kept_rows = [other for other in range(3) if other != row]
    kept_cols = [other for other in range(3) if other != col]
    first = matrix[kept_rows[0]][kept_cols[0]] * matrix[kept_rows[1]][kept_cols[1]]
    second = matrix[kept_rows[0]][kept_cols[1]] * matrix[kept_rows[1]][kept_cols[0]]
    return first - second if (row + col) % 2 == 0 else second - first


def rows_sum(block):
    return jnp.sum(block, axis=0, keepdims=True)


def total_of(block):
    return jnp.sum(rows_sum(block), axis=1, keepdims=True)


def pieces_of(block):
    upper = block.astype(jnp.bfloat16)
    lower = (block - upper.astype(jnp.float32)).astype(jnp.bfloat16)
    return upper, lower


def kernel(
    n,
    cam_ref,
    point_ref,
    resid_ref,
    ids_ref,
    damp_ref,
    camera_out,
    point_out,
    hot_ref,
    low_ref,
    jac_ref,
    inv_ref,
    pred_ref,
    remain_ref,
    table_ref,
    first_send,
    first_recv,
    part_send,
    part_recv,
    slice_send,
    slice_recv,
    scalar_send,
    scalar_recv,
    send_sems,
    recv_sems,
):
    me = lax.axis_index("pts")
    views, points = ids_ref.shape
    lanes = camera_out.shape[1]
    params = camera_out.shape[0]
    main = params - 1
    wide = 2 * lanes
    low = n // 2
    damp = damp_ref[0]
    barrier = pltpu.get_barrier_semaphore()

    def greet(step, carry):
        peer = lax.rem(me + 1 + step, n)
        pl.semaphore_signal(
            barrier, inc=1, device_id={"pts": peer}, device_id_type=pl.DeviceIdType.MESH
        )
        return carry

    lax.fori_loop(0, n - 1, greet, 0)

    def exchange(phase, source, target):
        def copy_to(peer, slot):
            return pltpu.make_async_remote_copy(
                src_ref=source(peer),
                dst_ref=target.at[slot],
                send_sem=send_sems.at[phase, peer],
                recv_sem=recv_sems.at[phase, slot],
                device_id={"pts": peer},
                device_id_type=pl.DeviceIdType.MESH,
            )

        def begin(step, carry):
            copy_to(lax.rem(me + 1 + step, n), me).start()
            return carry

        def end(step, carry):
            peer = lax.rem(me + 1 + step, n)
            copy = copy_to(peer, peer)
            copy.wait_recv()
            copy.wait_send()
            return carry

        lax.fori_loop(0, n - 1, begin, 0)
        lax.fori_loop(0, n - 1, end, 0)

    def spread(value):
        return jnp.broadcast_to(value, (1, lanes))

    for view in range(views):
        ids = ids_ref[view : view + 1, :]
        cols = pl.ds(view * points, points)
        lane_ids = lax.bitwise_and(ids, wide - 1) if wide & (wide - 1) == 0 else lax.rem(ids, wide)
        row_ids = (ids - lane_ids) // wide
        high = lax.broadcasted_iota(jnp.int32, (wide, points), 0) == lane_ids
        hot_ref[:, cols] = high.astype(jnp.float32).astype(jnp.bfloat16)
        lows = lax.broadcasted_iota(jnp.int32, (low, points), 0) == row_ids
        low_ref[:, cols] = lows.astype(jnp.float32)
    for coord in range(3):
        jac_ref[coord] = jnp.concatenate([point_ref[0, coord], point_ref[1, coord]], axis=0)

    gram = [[None] * 3 for unused in range(3)]
    for row in range(3):
        for col in range(row, 3):
            entry = rows_sum(jac_ref[row] * jac_ref[col])
            if row == col:
                entry = entry + damp
            gram[row][col] = entry
            gram[col][row] = entry
    determinant = (
        gram[0][0] * cofactor(gram, 0, 0)
        + gram[0][1] * cofactor(gram, 0, 1)
        + gram[0][2] * cofactor(gram, 0, 2)
    )
    for row in range(3):
        for col in range(3):
            inv_ref[3 * row + col : 3 * row + col + 1, :] = cofactor(gram, col, row) / determinant

    def solve(pulled):
        return [
            sum(inv_ref[3 * row + col : 3 * row + col + 1, :] * pulled[col] for col in range(3))
            for row in range(3)
        ]

    def pull(rows):
        return [rows_sum(jac_ref[coord] * rows) for coord in range(3)]

    def push(solved):
        return sum(jac_ref[coord] * solved[coord] for coord in range(3))

    def at_views(view):
        cols = pl.ds(view * points, points)
        return hot_ref[:, cols], low_ref[:, cols]

    def weigh(upper_rows, last_row, lows):
        stacked = [upper_rows * lows[row : row + 1, :] for row in range(low)]
        return jnp.concatenate(stacked + [last_row * lows], axis=0)

    def scatter(values_of):
        totals = None
        for view in range(views):
            hot, lows = at_views(view)
            found = []
            for upper_rows, last_row in values_of(view):
                upper, lower = pieces_of(weigh(upper_rows, last_row, lows))
                found.append(
                    lax.dot_general(upper, hot, NT, preferred_element_type=jnp.float32)
                    + lax.dot_general(lower, hot, NT, preferred_element_type=jnp.float32)
                )
            totals = found if totals is None else [a + b for a, b in zip(totals, found)]
        return totals

    def pulled_values(view):
        first = remain_ref[view : view + 1, :]
        second = remain_ref[views + view : views + view + 1, :]
        return (
            cam_ref[view, 0, 0:main, :] * first + cam_ref[view, 1, 0:main, :] * second,
            cam_ref[view, 0, main:params, :] * first + cam_ref[view, 1, main:params, :] * second,
        )

    def squares(view):
        first, second = cam_ref[view, 0], cam_ref[view, 1]
        both = first * first + second * second
        return both[0:main], both[main:params]

    def fill(target, totals, offset, last):
        for slot in range(n):
            row, half = slot // 2, (slot % 2) * lanes
            target[slot, offset : offset + main, :] = totals[
                row * main : (row + 1) * main, half : half + lanes
            ]
            target[slot, last : last + 1, :] = totals[
                low * main + row : low * main + row + 1, half : half + lanes
            ]

    resid = resid_ref[...]
    grad = pull(resid)
    remain_ref[...] = resid - push(solve(grad))
    right_part, diag_part = scatter(lambda view: [pulled_values(view), squares(view)])
    fill(first_send, -right_part, 0, 2 * main)
    fill(first_send, diag_part, main, 2 * main + 1)
    pl.semaphore_wait(barrier, n - 1)
    first_recv[me] = first_send[me]
    exchange(0, lambda peer: first_send.at[peer], first_recv)
    summed = jnp.sum(first_recv[...], axis=0)
    residual_vec = jnp.concatenate([summed[0:main], summed[2 * main : 2 * main + 1]], axis=0)
    precond = damp + jnp.concatenate(
        [summed[main : 2 * main], summed[2 * main + 1 : 2 * main + 2]], axis=0
    )
    phase = 1
    norm_now = None
    direction = None
    step_sum = None
    pulled_sum = grad
    for iteration in range(ITERS):
        scaled = residual_vec / precond
        slice_send[iteration, 0:params, :] = scaled
        slice_send[iteration, params : params + 1, :] = spread(total_of(residual_vec * scaled))
        mine = slice_recv.at[iteration]
        mine[me] = slice_send[iteration]
        exchange(phase, lambda peer: slice_send.at[iteration], mine)
        phase += 1
        norm_next = jnp.sum(mine[:, params, :], axis=0, keepdims=True)
        factor = None if norm_now is None else norm_next / norm_now
        norm_now = norm_next
        direction = scaled if factor is None else scaled + factor * direction
        for slot in range(n):
            row, half = slot // 2, (slot % 2) * lanes
            spots = (
                (slice(row * main, (row + 1) * main), slice(0, main)),
                (slice(low * main + row, low * main + row + 1), slice(main, params)),
            )
            for spot, source in spots:
                update = mine[slot, source, :]
                if factor is not None:
                    update = update + factor * table_ref[spot, half : half + lanes]
                table_ref[spot, half : half + lanes] = update
        lookup_upper, lookup_lower = pieces_of(table_ref[...])
        for view in range(views):
            hot, lows = at_views(view)
            picked = jnp.dot(lookup_upper, hot, preferred_element_type=jnp.float32) + jnp.dot(
                lookup_lower, hot, preferred_element_type=jnp.float32
            )
            upper_rows = sum(
                picked[row * main : (row + 1) * main] * lows[row : row + 1] for row in range(low)
            )
            last_row = rows_sum(picked[low * main :] * lows)
            for part in range(2):
                pred_ref[part * views + view : part * views + view + 1, :] = (
                    rows_sum(cam_ref[view, part, 0:main, :] * upper_rows)
                    + cam_ref[view, part, main:params, :] * last_row
                )
        predicted = pred_ref[...]
        pulled = pull(predicted)
        remain = predicted - push(solve(pulled))
        curve_part = spread(total_of(predicted * remain) + damp * total_of(direction * direction))
        if iteration + 1 < ITERS:
            remain_ref[...] = remain
            (image_part,) = scatter(lambda view: [pulled_values(view)])
            outgoing = part_send.at[iteration]
            incoming = part_recv.at[iteration]
            fill(outgoing, image_part, 0, main)
            for slot in range(n):
                outgoing[slot, params : params + 1, :] = curve_part
            incoming[me] = outgoing[me]
            exchange(phase, lambda peer: outgoing.at[peer], incoming)
            phase += 1
            summed = jnp.sum(incoming[...], axis=0)
            image = damp * direction + summed[0:params]
            curve = summed[params : params + 1]
        else:
            scalar_send[...] = curve_part
            scalar_recv[me] = curve_part
            exchange(phase, lambda peer: scalar_send, scalar_recv)
            curve = jnp.sum(scalar_recv[...], axis=0)
        step_size = norm_now / curve
        moved = step_size * direction
        step_sum = moved if step_sum is None else step_sum + moved
        wide_step = jnp.concatenate([step_size] * (points // lanes), axis=1)
        pulled_sum = [old + wide_step * new for old, new in zip(pulled_sum, pulled)]
        if iteration + 1 < ITERS:
            residual_vec = residual_vec - step_size * image
    camera_out[...] = step_sum
    solved = solve(pulled_sum)
    for coord in range(3):
        point_out[coord : coord + 1, :] = -solved[coord]


def body(n, cam_jac, point_jac, residuals, obs_camera, damping):
    params = cam_jac.shape[1]
    views, points = obs_camera.shape
    lanes = NCAM // n
    wide, low = 2 * lanes, n // 2
    main = params - 1
    phases = 2 * ITERS + 1
    vmem = functools.partial(pl.BlockSpec, memory_space=pltpu.VMEM)
    return pl.pallas_call(
        functools.partial(kernel, n),
        name="schur_solve",
        out_shape=(
            jax.ShapeDtypeStruct((params, lanes), jnp.float32),
            jax.ShapeDtypeStruct((3, points), jnp.float32),
        ),
        in_specs=[vmem(), vmem(), vmem(), vmem(), pl.BlockSpec(memory_space=pltpu.SMEM)],
        out_specs=(vmem(), vmem()),
        scratch_shapes=[
            pltpu.VMEM((wide, views * points), jnp.bfloat16),
            pltpu.VMEM((low, views * points), jnp.float32),
            pltpu.VMEM((3, 2 * views, points), jnp.float32),
            pltpu.VMEM((9, points), jnp.float32),
            pltpu.VMEM((2 * views, points), jnp.float32),
            pltpu.VMEM((2 * views, points), jnp.float32),
            pltpu.VMEM((low * params, wide), jnp.float32),
            pltpu.VMEM((n, 2 * params, lanes), jnp.float32),
            pltpu.VMEM((n, 2 * params, lanes), jnp.float32),
            pltpu.VMEM((ITERS - 1, n, params + 1, lanes), jnp.float32),
            pltpu.VMEM((ITERS - 1, n, params + 1, lanes), jnp.float32),
            pltpu.VMEM((ITERS, params + 1, lanes), jnp.float32),
            pltpu.VMEM((ITERS, n, params + 1, lanes), jnp.float32),
            pltpu.VMEM((1, lanes), jnp.float32),
            pltpu.VMEM((n, 1, lanes), jnp.float32),
            pltpu.SemaphoreType.DMA((phases, n)),
            pltpu.SemaphoreType.DMA((phases, n)),
        ],
        compiler_params=pltpu.CompilerParams(collective_id=0, has_side_effects=True),
    )(
        cam_jac.transpose(2, 0, 1, 3),
        point_jac,
        residuals.reshape(2 * views, points),
        obs_camera,
        damping,
    )


def solution(mesh):
    in_specs = (
        P(None, None, None, ("sub", "pts")),
        P(None, None, None, ("sub", "pts")),
        P(None, None, ("sub", "pts")),
        P(None, ("sub", "pts")),
        P("sub"),
    )
    out_specs = (P(None, ("sub", "pts")), P(None, ("sub", "pts")))
    return jax.shard_map(
        functools.partial(body, mesh.shape["pts"]),
        mesh=mesh,
        in_specs=in_specs,
        out_specs=out_specs,
        check_vma=False,
    )
```

time: 603 us -> 72.7 us (0.12)
  waiting for transfers between devices: 509 us -> 0 us
  Pallas kernels: 0 us -> 65.9 us
  matrix products: 26.7 us -> 0 us
  other arithmetic: 23.2 us -> 0 us
  between operations: 21.5 us -> 1.29 us
  local copies, waits for them, and re-layouts: 17.1 us -> 5.22 us
    psum x4 -> x0, waiting for transfers between devices: 509 us -> none  [the longest x3 377 us: body(): lax.psum(schur_terms(direction, cam_jac, point_jac, obs_camera, inverse,...]
    pallas_call x0 -> x1, Pallas kernels: none -> 65.9 us  [body(): pl.pallas_call(functools.partial(kernel, n), name='schur_solve', out_shap...]
    dot_general x64 -> x0, matrix products: 26.7 us -> none  [the longest x32 16 us: add_block(): lax.dot_general(weighted, hot_high, (((1,), (1,)), ((), ())), precision=l...]
    reduce_sum x60 -> x0, other arithmetic: 15.3 us -> none  [the longest x3 5.1 us: body(): step_size = norm_now / jnp.sum(direction * image)]
    reshape x15 -> x1, local copies, waits for them, and re-layouts: 7.9 us -> 1.38 us  [body(): residuals.reshape(2 * views, points)]
  transfers between devices with their start and end apart: 4 -> 0, of which waited for: 4 -> 0; matrix products, arithmetic and copies ran while one was open for 0% -> 0% of each run, Pallas kernels for 0% -> 0%
where the time goes in v1:
time: 72.7 us; the launch traced here: 72.4 us
  Pallas kernels  65.9 us (91%)
  local copies, waits for them, and re-layouts  5.22 us (7%)
  between operations  1.29 us (2%)
    pallas_call x1, Pallas kernels, body(): pl.pallas_call(functools.partial(kernel, n), name='schur_solve', out_shap...  65.9 us
    unnamed x5, local copies, waits for them, and re-layouts  3.84 us

profile of v1, /device:TPU:0, one launch (start us, length us, event | category | flops | bytes accessed | tf_op | source)
XLA Modules:
  0.0 72.4 jit_solution(15513304579465917787)
XLA Ops:
  1.3 1.4 %reshape.7.resid_ref = f32[8,1024]{1,0:T(8,128)} reshape(f32[2,4,1024]{2,1,0:T(4,128)} %param.7) | data formatting | bytes 65536 | tf_op jit(solution)/shard_map/reshape | solution.py:330
  2.7 1.9 %copy.9 = f32[2,9,4,1024]{3,1,0,2:T(8,128)} copy(f32[2,9,4,1024]{3,2,1,0:T(4,128)} %param.5) | data formatting | bytes 589824 | tf_op args[0]
  4.6 65.9 %schur_solve.1 = (f32[9,128]{1,0:T(8,128)}, f32[3,1024]{1,0:T(4,128)}) custom-call(f32[4,2,9,1024]{3,2,1,0:T(8,128)} %bitcast.3, f32[2,3,4,1024]{3,2,1,0:T(4,128)} %point_ref.1, f32[8,1024]{1,0:T(8,128)} %reshape.7.resid_ref, s32[4,1024]{1,0:T(4,128)} %ids_ref.1, f32[1]{0:T(128)S(6)} %copy.12.damp_ref), custom_call_target="tpu_custom_call" | custom-call | tf_op jit(solution)/shard_map/schur_solve/pallas_call | solution.py:298
  70.5 0.0 copy-start
  70.5 1.3 %copy.13 = f32[9,128]{1,0:T(8,128)} copy(f32[9,128]{1,0:T(8,128)} %get-tuple-element.4) | data formatting | bytes 9216
  71.8 0.0 copy-done
  71.8 0.6 copy.14
Async XLA Ops:
  70.5 1.3 %copy-start = (f32[3,1024]{1,0:T(4,128)S(1)}, f32[3,1024]{1,0:T(4,128)}, u32[]{:S(2)}) copy-start(f32[3,1024]{1,0:T(4,128)} %get-tuple-element.5) | copy-start | bytes 36868

commit v2 on v1

--- a/solution.py
+++ b/solution.py
@@ -28,21 +28,21 @@
     return jnp.sum(rows_sum(block), axis=1, keepdims=True)
 
 
-def pieces_of(block):
-    upper = block.astype(jnp.bfloat16)
-    lower = (block - upper.astype(jnp.float32)).astype(jnp.bfloat16)
-    return upper, lower
+def halves_of(block):
+    upper = block.astype(jnp.bfloat16).astype(jnp.float32)
+    return upper, block - upper
 
 
 def kernel(
     n,
-    cam_ref,
+    cam_given,
     point_ref,
     resid_ref,
     ids_ref,
     damp_ref,
     camera_out,
     point_out,
+    cam_ref,
     hot_ref,
     low_ref,
     jac_ref,
@@ -70,6 +70,7 @@
     low = n // 2
     damp = damp_ref[0]
     barrier = pltpu.get_barrier_semaphore()
+    sent = []
 
     def greet(step, carry):
         peer = lax.rem(me + 1 + step, n)
@@ -81,29 +82,22 @@
     lax.fori_loop(0, n - 1, greet, 0)
 
     def exchange(phase, source, target):
-        def copy_to(peer, slot):
-            return pltpu.make_async_remote_copy(
+        def begin(step, carry):
+            peer = lax.rem(me + 1 + lax.rem(step + n // 4, n - 1), n)
+            pltpu.make_async_remote_copy(
                 src_ref=source(peer),
-                dst_ref=target.at[slot],
-                send_sem=send_sems.at[phase, peer],
-                recv_sem=recv_sems.at[phase, slot],
+                dst_ref=target.at[me],
+                send_sem=send_sems.at[phase],
+                recv_sem=recv_sems.at[phase],
                 device_id={"pts": peer},
                 device_id_type=pl.DeviceIdType.MESH,
-            )
-
-        def begin(step, carry):
-            copy_to(lax.rem(me + 1 + step, n), me).start()
+            ).start()
             return carry
 
-        def end(step, carry):
-            peer = lax.rem(me + 1 + step, n)
-            copy = copy_to(peer, peer)
-            copy.wait_recv()
-            copy.wait_send()
-            return carry
-
         lax.fori_loop(0, n - 1, begin, 0)
-        lax.fori_loop(0, n - 1, end, 0)
+        others = target.at[pl.ds(0, n - 1)]
+        sent.append(pltpu.make_async_copy(others, others, send_sems.at[phase]))
+        pltpu.make_async_copy(others, others, recv_sems.at[phase]).wait()
 
     def spread(value):
         return jnp.broadcast_to(value, (1, lanes))
@@ -116,7 +110,10 @@
         high = lax.broadcasted_iota(jnp.int32, (wide, points), 0) == lane_ids
         hot_ref[:, cols] = high.astype(jnp.float32).astype(jnp.bfloat16)
         lows = lax.broadcasted_iota(jnp.int32, (low, points), 0) == row_ids
-        low_ref[:, cols] = lows.astype(jnp.float32)
+        low_ref[:, cols] = lows.astype(jnp.float32).astype(jnp.bfloat16)
+    for view in range(views):
+        for part in range(2):
+            cam_ref[view, part] = cam_given[part, :, view, :]
     for coord in range(3):
         jac_ref[coord] = jnp.concatenate([point_ref[0, coord], point_ref[1, coord]], axis=0)
 
@@ -153,22 +150,19 @@
         cols = pl.ds(view * points, points)
         return hot_ref[:, cols], low_ref[:, cols]
 
-    def weigh(upper_rows, last_row, lows):
-        stacked = [upper_rows * lows[row : row + 1, :] for row in range(low)]
-        return jnp.concatenate(stacked + [last_row * lows], axis=0)
-
     def scatter(values_of):
         totals = None
         for view in range(views):
             hot, lows = at_views(view)
-            found = []
+            stacked = []
             for upper_rows, last_row in values_of(view):
-                upper, lower = pieces_of(weigh(upper_rows, last_row, lows))
-                found.append(
-                    lax.dot_general(upper, hot, NT, preferred_element_type=jnp.float32)
-                    + lax.dot_general(lower, hot, NT, preferred_element_type=jnp.float32)
-                )
-            totals = found if totals is None else [a + b for a, b in zip(totals, found)]
+                both = jnp.concatenate(halves_of(upper_rows), axis=0).astype(jnp.bfloat16)
+                stacked += [both * lows[row : row + 1, :] for row in range(low)]
+                stacked += [half.astype(jnp.bfloat16) * lows for half in halves_of(last_row)]
+            found = lax.dot_general(
+                jnp.concatenate(stacked, axis=0), hot, NT, preferred_element_type=jnp.float32
+            )
+            totals = found if totals is None else totals + found
         return totals
 
     def pulled_values(view):
@@ -184,22 +178,23 @@
         both = first * first + second * second
         return both[0:main], both[main:params]
 
-    def fill(target, totals, offset, last):
+    def fill(target, totals, start, offset, last, sign):
         for slot in range(n):
             row, half = slot // 2, (slot % 2) * lanes
-            target[slot, offset : offset + main, :] = totals[
-                row * main : (row + 1) * main, half : half + lanes
-            ]
-            target[slot, last : last + 1, :] = totals[
-                low * main + row : low * main + row + 1, half : half + lanes
-            ]
-
-    resid = resid_ref[...]
+            cols = slice(half, half + lanes)
+            first = start + 2 * main * row
+            upper = totals[first : first + main, cols] + totals[first + main : first + 2 * main, cols]
+            first = start + 2 * main * low + row
+            lower = totals[first : first + 1, cols] + totals[first + low : first + low + 1, cols]
+            target[slot, offset : offset + main, :] = upper if sign > 0 else -upper
+            target[slot, last : last + 1, :] = lower if sign > 0 else -lower
+
+    resid = jnp.concatenate([resid_ref[0], resid_ref[1]], axis=0)
     grad = pull(resid)
     remain_ref[...] = resid - push(solve(grad))
-    right_part, diag_part = scatter(lambda view: [pulled_values(view), squares(view)])
-    fill(first_send, -right_part, 0, 2 * main)
-    fill(first_send, diag_part, main, 2 * main + 1)
+    both_parts = scatter(lambda view: [pulled_values(view), squares(view)])
+    fill(first_send, both_parts, 0, 0, 2 * main, -1)
+    fill(first_send, both_parts, 2 * low * params, main, 2 * main + 1, 1)
     pl.semaphore_wait(barrier, n - 1)
     first_recv[me] = first_send[me]
     exchange(0, lambda peer: first_send.at[peer], first_recv)
@@ -236,16 +231,19 @@
                 if factor is not None:
                     update = update + factor * table_ref[spot, half : half + lanes]
                 table_ref[spot, half : half + lanes] = update
-        lookup_upper, lookup_lower = pieces_of(table_ref[...])
+        upper, lower = halves_of(table_ref[...])
+        lookup = jnp.concatenate([upper, lower], axis=0).astype(jnp.bfloat16)
         for view in range(views):
             hot, lows = at_views(view)
-            picked = jnp.dot(lookup_upper, hot, preferred_element_type=jnp.float32) + jnp.dot(
-                lookup_lower, hot, preferred_element_type=jnp.float32
+            lows = lows.astype(jnp.float32)
+            picked = jnp.dot(lookup, hot, preferred_element_type=jnp.float32)
+            size = low * params
+            upper_rows = sum(
+                (picked[row * main : (row + 1) * main] + picked[size + row * main : size + (row + 1) * main])
+                * lows[row : row + 1]
+                for row in range(low)
             )
-            upper_rows = sum(
-                picked[row * main : (row + 1) * main] * lows[row : row + 1] for row in range(low)
-            )
-            last_row = rows_sum(picked[low * main :] * lows)
+            last_row = rows_sum((picked[low * main : size] + picked[size + low * main :]) * lows)
             for part in range(2):
                 pred_ref[part * views + view : part * views + view + 1, :] = (
                     rows_sum(cam_ref[view, part, 0:main, :] * upper_rows)
@@ -257,10 +255,10 @@
         curve_part = spread(total_of(predicted * remain) + damp * total_of(direction * direction))
         if iteration + 1 < ITERS:
             remain_ref[...] = remain
-            (image_part,) = scatter(lambda view: [pulled_values(view)])
+            image_part = scatter(lambda view: [pulled_values(view)])
             outgoing = part_send.at[iteration]
             incoming = part_recv.at[iteration]
-            fill(outgoing, image_part, 0, main)
+            fill(outgoing, image_part, 0, 0, main, 1)
             for slot in range(n):
                 outgoing[slot, params : params + 1, :] = curve_part
             incoming[me] = outgoing[me]
@@ -282,6 +280,8 @@
         if iteration + 1 < ITERS:
             residual_vec = residual_vec - step_size * image
     camera_out[...] = step_sum
+    for copy in sent:
+        copy.wait()
     solved = solve(pulled_sum)
     for coord in range(3):
         point_out[coord : coord + 1, :] = -solved[coord]
@@ -305,8 +305,9 @@
         in_specs=[vmem(), vmem(), vmem(), vmem(), pl.BlockSpec(memory_space=pltpu.SMEM)],
         out_specs=(vmem(), vmem()),
         scratch_shapes=[
+            pltpu.VMEM((views, 2, params, points), jnp.float32),
             pltpu.VMEM((wide, views * points), jnp.bfloat16),
-            pltpu.VMEM((low, views * points), jnp.float32),
+            pltpu.VMEM((low, views * points), jnp.bfloat16),
             pltpu.VMEM((3, 2 * views, points), jnp.float32),
             pltpu.VMEM((9, points), jnp.float32),
             pltpu.VMEM((2 * views, points), jnp.float32),
@@ -320,14 +321,14 @@
             pltpu.VMEM((ITERS, n, params + 1, lanes), jnp.float32),
             pltpu.VMEM((1, lanes), jnp.float32),
             pltpu.VMEM((n, 1, lanes), jnp.float32),
-            pltpu.SemaphoreType.DMA((phases, n)),
-            pltpu.SemaphoreType.DMA((phases, n)),
+            pltpu.SemaphoreType.DMA((phases,)),
+            pltpu.SemaphoreType.DMA((phases,)),
         ],
         compiler_params=pltpu.CompilerParams(collective_id=0, has_side_effects=True),
     )(
-        cam_jac.transpose(2, 0, 1, 3),
+        cam_jac,
         point_jac,
-        residuals.reshape(2 * views, points),
+        residuals,
         obs_camera,
         damping,
     )

time: 72.7 us -> 62.9 us (0.87)
  Pallas kernels: 65.9 us -> 59.5 us
  local copies, waits for them, and re-layouts: 5.22 us -> 1.91 us
    pallas_call x1, Pallas kernels: 65.9 us -> 59.5 us  [body(): pl.pallas_call(functools.partial(kernel, n), name='schur_solve', out_shap...]
    unnamed x5 -> x4, local copies, waits for them, and re-layouts: 3.84 us -> 1.91 us
    reshape x1 -> x0, local copies, waits for them, and re-layouts: 1.38 us -> none  [body(): residuals.reshape(2 * views, points)]
where the time goes in v2:
time: 62.9 us; the launch traced here: 62.7 us
  Pallas kernels  59.5 us (95%)
  local copies, waits for them, and re-layouts  1.91 us (3%)
  between operations  1.29 us (2%)
    pallas_call x1, Pallas kernels, body(): pl.pallas_call(functools.partial(kernel, n), name='schur_solve', out_shap...  59.5 us
    unnamed x4, local copies, waits for them, and re-layouts  1.91 us

profile of v2, /device:TPU:0, one launch (start us, length us, event | category | flops | bytes accessed | tf_op | source)
XLA Modules:
  0.0 62.7 jit_solution(12949363715953274160)
XLA Ops:
  1.3 59.5 %schur_solve.1 = (f32[9,128]{1,0:T(8,128)}, f32[3,1024]{1,0:T(4,128)}) custom-call(f32[2,9,4,1024]{3,2,1,0:T(4,128)} %cam_given.1, f32[2,3,4,1024]{3,2,1,0:T(4,128)} %point_ref.1, f32[2,4,1024]{2,1,0:T(4,128)} %resid_ref.1, s32[4,1024]{1,0:T(4,128)} %ids_ref.1, f32[1]{0:T(128)S(6)} %copy.9.damp_ref), custom_call_target="tpu_custom_call" | custom-call | tf_op jit(solution)/shard_map/schur_solve/pallas_call | solution.py:298
  60.8 0.0 copy-start
  60.8 1.3 %copy.10 = f32[9,128]{1,0:T(8,128)} copy(f32[9,128]{1,0:T(8,128)} %get-tuple-element.4) | data formatting | bytes 9216
  62.1 0.0 copy-done
  62.1 0.6 copy.11
Async XLA Ops:
  60.8 1.3 %copy-start = (f32[3,1024]{1,0:T(4,128)S(1)}, f32[3,1024]{1,0:T(4,128)}, u32[]{:S(2)}) copy-start(f32[3,1024]{1,0:T(4,128)} %get-tuple-element.5) | copy-start | bytes 36868

commit v3 on v2

--- a/solution.py
+++ b/solution.py
@@ -9,6 +9,7 @@
 
 NCAM = 4096
 ITERS = 3
+GROUP = 4
 NT = (((1,), (1,)), ((), ()))
 
 
@@ -35,10 +36,10 @@
 
 def kernel(
     n,
-    cam_given,
-    point_ref,
-    resid_ref,
-    ids_ref,
+    cam_far,
+    point_far,
+    resid_far,
+    ids_far,
     damp_ref,
     camera_out,
     point_out,
@@ -58,6 +59,11 @@
     slice_recv,
     scalar_send,
     scalar_recv,
+    cam_given,
+    point_ref,
+    resid_ref,
+    ids_ref,
+    load_sems,
     send_sems,
     recv_sems,
 ):
@@ -66,8 +72,8 @@
     lanes = camera_out.shape[1]
     params = camera_out.shape[0]
     main = params - 1
-    wide = 2 * lanes
-    low = n // 2
+    wide = GROUP * lanes
+    low = n // GROUP
     damp = damp_ref[0]
     barrier = pltpu.get_barrier_semaphore()
     sent = []
@@ -80,10 +86,19 @@
         return carry
 
     lax.fori_loop(0, n - 1, greet, 0)
+    far = (ids_far, cam_far, point_far, resid_far)
+    near = (ids_ref, cam_given, point_ref, resid_ref)
+    loads = [
+        pltpu.make_async_copy(source, target, load_sems.at[spot])
+        for spot, (source, target) in enumerate(zip(far, near))
+    ]
+    for load in loads:
+        load.start()
+    loads[0].wait()
 
     def exchange(phase, source, target):
         def begin(step, carry):
-            peer = lax.rem(me + 1 + lax.rem(step + n // 4, n - 1), n)
+            peer = lax.rem(me + 1 + step, n)
             pltpu.make_async_remote_copy(
                 src_ref=source(peer),
                 dst_ref=target.at[me],
@@ -111,6 +126,8 @@
         hot_ref[:, cols] = high.astype(jnp.float32).astype(jnp.bfloat16)
         lows = lax.broadcasted_iota(jnp.int32, (low, points), 0) == row_ids
         low_ref[:, cols] = lows.astype(jnp.float32).astype(jnp.bfloat16)
+    for load in loads[1:]:
+        load.wait()
     for view in range(views):
         for part in range(2):
             cam_ref[view, part] = cam_given[part, :, view, :]
@@ -180,7 +197,7 @@
 
     def fill(target, totals, start, offset, last, sign):
         for slot in range(n):
-            row, half = slot // 2, (slot % 2) * lanes
+            row, half = slot // GROUP, (slot % GROUP) * lanes
             cols = slice(half, half + lanes)
             first = start + 2 * main * row
             upper = totals[first : first + main, cols] + totals[first + main : first + 2 * main, cols]
@@ -221,7 +238,7 @@
         norm_now = norm_next
         direction = scaled if factor is None else scaled + factor * direction
         for slot in range(n):
-            row, half = slot // 2, (slot % 2) * lanes
+            row, half = slot // GROUP, (slot % GROUP) * lanes
             spots = (
                 (slice(row * main, (row + 1) * main), slice(0, main)),
                 (slice(low * main + row, low * main + row + 1), slice(main, params)),
@@ -284,25 +301,30 @@
         copy.wait()
     solved = solve(pulled_sum)
     for coord in range(3):
-        point_out[coord : coord + 1, :] = -solved[coord]
+        point_out[coord : coord + 1, :] = solved[coord]
+
+
+def hand_on(camera_ref, point_ref, camera_out, point_out):
+    camera_out[...] = camera_ref[...]
+    point_out[...] = -point_ref[...]
 
 
 def body(n, cam_jac, point_jac, residuals, obs_camera, damping):
     params = cam_jac.shape[1]
     views, points = obs_camera.shape
     lanes = NCAM // n
-    wide, low = 2 * lanes, n // 2
+    wide, low = GROUP * lanes, n // GROUP
     main = params - 1
     phases = 2 * ITERS + 1
     vmem = functools.partial(pl.BlockSpec, memory_space=pltpu.VMEM)
-    return pl.pallas_call(
+    camera_step, point_step = pl.pallas_call(
         functools.partial(kernel, n),
         name="schur_solve",
         out_shape=(
             jax.ShapeDtypeStruct((params, lanes), jnp.float32),
             jax.ShapeDtypeStruct((3, points), jnp.float32),
         ),
-        in_specs=[vmem(), vmem(), vmem(), vmem(), pl.BlockSpec(memory_space=pltpu.SMEM)],
+        in_specs=[pl.BlockSpec(memory_space=pl.ANY)] * 4 + [pl.BlockSpec(memory_space=pltpu.SMEM)],
         out_specs=(vmem(), vmem()),
         scratch_shapes=[
             pltpu.VMEM((views, 2, params, points), jnp.float32),
@@ -321,6 +343,11 @@
             pltpu.VMEM((ITERS, n, params + 1, lanes), jnp.float32),
             pltpu.VMEM((1, lanes), jnp.float32),
             pltpu.VMEM((n, 1, lanes), jnp.float32),
+            pltpu.VMEM(cam_jac.shape, jnp.float32),
+            pltpu.VMEM(point_jac.shape, jnp.float32),
+            pltpu.VMEM(residuals.shape, jnp.float32),
+            pltpu.VMEM(obs_camera.shape, jnp.int32),
+            pltpu.SemaphoreType.DMA((4,)),
             pltpu.SemaphoreType.DMA((phases,)),
             pltpu.SemaphoreType.DMA((phases,)),
         ],
@@ -332,6 +359,16 @@
         obs_camera,
         damping,
     )
+    return pl.pallas_call(
+        hand_on,
+        name="hand_on",
+        out_shape=(
+            jax.ShapeDtypeStruct(camera_step.shape, jnp.float32),
+            jax.ShapeDtypeStruct(point_step.shape, jnp.float32),
+        ),
+        in_specs=[vmem(), vmem()],
+        out_specs=(vmem(), vmem()),
+    )(camera_step, point_step)
 
 
 def solution(mesh):

time: 62.9 us -> 60 us (0.954)
  local copies, waits for them, and re-layouts: 1.91 us -> 0 us
  Pallas kernels: 59.5 us -> 58.4 us
    pallas_call x1, Pallas kernels: 59.5 us -> 57 us  [body(): pl.pallas_call(functools.partial(kernel, n), name='schur_solve', out_shap...]
    unnamed x4 -> x0, local copies, waits for them, and re-layouts: 1.91 us -> none
    pallas_call x0 -> x1, Pallas kernels: none -> 1.35 us  [body(): pl.pallas_call(hand_on, name='hand_on', out_shape=(jax.ShapeDtypeStruct(c...]
where the time goes in v3:
time: 60 us; the launch traced here: 59.7 us
  Pallas kernels  58.4 us (97%)
  between operations  1.29 us (2%)
    pallas_call x1, Pallas kernels, body(): pl.pallas_call(functools.partial(kernel, n), name='schur_solve', out_shap...  57 us
    pallas_call x1, Pallas kernels, body(): pl.pallas_call(hand_on, name='hand_on', out_shape=(jax.ShapeDtypeStruct(c...  1.35 us

profile of v3, /device:TPU:0, one launch (start us, length us, event | category | flops | bytes accessed | tf_op | source)
XLA Modules:
  0.0 59.7 jit_solution(16153025854022188154)
XLA Ops:
  1.3 57.0 %schur_solve.1 = (f32[9,128]{1,0:T(8,128)}, f32[3,1024]{1,0:T(4,128)}) custom-call(f32[2,9,4,1024]{3,2,1,0:T(4,128)} %cam_far.1, f32[2,3,4,1024]{3,2,1,0:T(4,128)} %point_far.1, f32[2,4,1024]{2,1,0:T(4,128)} %resid_far.1, s32[4,1024]{1,0:T(4,128)} %ids_far.1, f32[1]{0:T(128)S(6)} %copy.7.damp_ref), custom_call_target="tpu_custom_call" | custom-call | tf_op jit(solution)/shard_map/schur_solve/pallas_call | solution.py:320
  58.3 1.3 %hand_on.1 = (f32[9,128]{1,0:T(8,128)}, f32[3,1024]{1,0:T(4,128)}) custom-call(f32[9,128]{1,0:T(8,128)} %get-tuple-element.4.camera_ref, f32[3,1024]{1,0:T(4,128)} %get-tuple-element.5.point_ref), custom_call_target="tpu_custom_call" | custom-call | tf_op jit(solution)/shard_map/hand_on/pallas_call | solution.py:362

commit v4 on v3

--- a/solution.py
+++ b/solution.py
@@ -85,7 +85,7 @@
         )
         return carry
 
-    lax.fori_loop(0, n - 1, greet, 0)
+    lax.fori_loop(0, n - 1, greet, 0, unroll=True)
     far = (ids_far, cam_far, point_far, resid_far)
     near = (ids_ref, cam_given, point_ref, resid_ref)
     loads = [
@@ -109,7 +109,7 @@
             ).start()
             return carry
 
-        lax.fori_loop(0, n - 1, begin, 0)
+        lax.fori_loop(0, n - 1, begin, 0, unroll=True)
         others = target.at[pl.ds(0, n - 1)]
         sent.append(pltpu.make_async_copy(others, others, send_sems.at[phase]))
         pltpu.make_async_copy(others, others, recv_sems.at[phase]).wait()

time: 60 us -> 59.8 us (level)
  no operation moved by 1% of the time
where the time goes in v4:
time: 59.8 us; the launch traced here: 59.5 us
  Pallas kernels  58.2 us (97%)
  between operations  1.29 us (2%)
    pallas_call x1, Pallas kernels, body(): pl.pallas_call(functools.partial(kernel, n), name='schur_solve', out_shap...  56.9 us
    pallas_call x1, Pallas kernels, body(): pl.pallas_call(hand_on, name='hand_on', out_shape=(jax.ShapeDtypeStruct(c...  1.35 us

profile of v4, /device:TPU:0, one launch (start us, length us, event | category | flops | bytes accessed | tf_op | source)
XLA Modules:
  0.0 59.5 jit_solution(12420897882037533074)
XLA Ops:
  1.3 56.9 %schur_solve.1 = (f32[9,128]{1,0:T(8,128)}, f32[3,1024]{1,0:T(4,128)}) custom-call(f32[2,9,4,1024]{3,2,1,0:T(4,128)} %cam_far.1, f32[2,3,4,1024]{3,2,1,0:T(4,128)} %point_far.1, f32[2,4,1024]{2,1,0:T(4,128)} %resid_far.1, s32[4,1024]{1,0:T(4,128)} %ids_far.1, f32[1]{0:T(128)S(6)} %copy.7.damp_ref), custom_call_target="tpu_custom_call" | custom-call | tf_op jit(solution)/shard_map/schur_solve/pallas_call | solution.py:320
  58.2 1.3 %hand_on.1 = (f32[9,128]{1,0:T(8,128)}, f32[3,1024]{1,0:T(4,128)}) custom-call(f32[9,128]{1,0:T(8,128)} %get-tuple-element.4.camera_ref, f32[3,1024]{1,0:T(4,128)} %get-tuple-element.5.point_ref), custom_call_target="tpu_custom_call" | custom-call | tf_op jit(solution)/shard_map/hand_on/pallas_call | solution.py:362
